TPU v7x, 256 devices: a whole 4x4x8 slice. The times are simulated.
256 devices in a mesh: row: 8 (over x, core), col: 32 (over y, z).
Axes of the slice: x: 4, y: 4, z: 8, core: 2. Of those that a mesh axis runs over, the one named last changes fastest.
Arguments:
- frames: bfloat16 [3072, 4096], P('row', 'col'), may hold values from -6 to 6
- gain: float32 [4096], replicated, may hold values from 0.3 to 10
- w_value: bfloat16 [4096, 4096], P('row', 'col'), may hold values from -0.09375 to 0.09375
- w_gate: bfloat16 [4096, 4096], P('row', 'col'), may hold values from -0.09375 to 0.09375
- kernel: float32 [31, 4096], P(None, 'col'), may hold values from -1.5 to 1.5
- bias: float32 [4096], P('col'), may hold values from -3 to 3
- w_out: bfloat16 [4096, 4096], P('row', 'col'), may hold values from -0.09375 to 0.09375
- grad_out: bfloat16 [3072, 4096], P('row', 'col'), may hold values from -6 to 6
Outputs:
- encoded: bfloat16 [3072, 4096], P('row', 'col')
- input_grad: bfloat16 [3072, 4096], P('row', 'col')
- grad_value: float32 [4096, 4096], P('row', 'col')
- grad_gate: float32 [4096, 4096], P('row', 'col')
- grad_kernel: float32 [31, 4096], P(None, 'col')
- grad_bias: float32 [4096], P('col')
- grad_out_weight: float32 [4096, 4096], P('row', 'col')
- grad_gain: float32 [4096], P('col')
All inputs are finite; a program needn't handle non-finite values.
Results may differ from a plain program's by a relative error of at most 0.035.
Values may be sent and summed in bfloat16 or wider, within the bound.
No kernel may reach another device: no remote copies, remote signals or barrier semaphores. Data moves between devices by JAX's collectives and lax.ppermute only.
A program may use at most 128 MiB of HBM per device.

v0:
```python
import jax
import jax.numpy as jnp
from jax import lax
from jax.sharding import PartitionSpec as P

K = 31
LEN = 2048
epsilon = 1e-05


def extended(block, sides, width):
    for axis, dim in sides:
        count = lax.axis_size(axis)
        forward = [(i, i + 1) for i in range(count - 1)]
        backward = [(target, source) for source, target in forward]
        low = lax.ppermute(
            lax.slice_in_dim(block, block.shape[dim] - width, None, axis=dim), axis, forward
        )
        high = lax.ppermute(lax.slice_in_dim(block, 0, width, axis=dim), axis, backward)
        block = jnp.concatenate([low, block, high], axis=dim)
    return block


def tap_masks(positions):
    offsets = jnp.arange(K, dtype=jnp.int32) - K // 2
    placed = (positions % LEN)[None, :] + offsets[:, None]
    return ((placed >= 0) & (placed < LEN)).astype(jnp.float32)


def contract_rows(left, right):
    return lax.dot_general(
        left, right, (((0,), (0,)), ((), ())), preferred_element_type=jnp.float32
    )


def contract_cols(left, right):
    return lax.dot_general(
        left, right, (((1,), (1,)), ((), ())), preferred_element_type=jnp.float32
    )


def shards(frames, gain, w_value, w_gate, kernel, bias, w_out, grad_out):
    row_count = frames.shape[0]
    col_count = frames.shape[1]
    chan_count = w_value.shape[1]
    width = col_count * lax.axis_size("col")
    half_width = K // 2
    row_start = lax.axis_index("row") * row_count
    col_start = lax.axis_index("col") * col_count
    local_gain = lax.dynamic_slice_in_dim(gain, col_start, col_count, 0)
    wide = frames.astype(jnp.float32)
    sum_row, square_sum = lax.psum((jnp.sum(wide, axis=1), jnp.sum(wide * wide, axis=1)), "col")
    mean_row = sum_row / width
    inv_std = lax.rsqrt(square_sum / width - mean_row * mean_row + epsilon)
    centred = (wide - mean_row[:, None]) * inv_std[:, None]
    normed = lax.all_gather(
        (centred * local_gain[None, :]).astype(jnp.bfloat16), "col", axis=1, tiled=True
    )
    value_full, gate_full = (
        lax.all_gather(w_value, "row", axis=0, tiled=True),
        lax.all_gather(w_gate, "row", axis=0, tiled=True),
    )
    value_pre = jnp.dot(normed, value_full, preferred_element_type=jnp.float32)
    gate_pre = jnp.dot(normed, gate_full, preferred_element_type=jnp.float32)
    gate_sig = jax.nn.sigmoid(gate_pre)
    gated = (value_pre * gate_sig).astype(jnp.bfloat16)
    padded_glu = extended(gated, (("row", 0),), half_width).astype(jnp.float32)
    local_masks = tap_masks(row_start + jnp.arange(row_count, dtype=jnp.int32))
    conv_pre = jnp.zeros((row_count, chan_count), jnp.float32) + bias[None, :]
    for tap_index in range(K):
        conv_pre = (
            conv_pre
            + kernel[tap_index][None, :]
            * local_masks[tap_index][:, None]
            * padded_glu[tap_index : tap_index + row_count]
        )
    conv_sig = jax.nn.sigmoid(conv_pre)
    activated = (conv_pre * conv_sig).astype(jnp.bfloat16)
    act_full = lax.all_gather(activated, "col", axis=1, tiled=True)
    out_full = lax.all_gather(w_out, "row", axis=0, tiled=True)
    encoded = (
        frames.astype(jnp.float32) + jnp.dot(act_full, out_full, preferred_element_type=jnp.float32)
    ).astype(jnp.bfloat16)
    act_terms = contract_cols(grad_out, out_full)
    act_grad = lax.psum_scatter(
        act_terms.astype(jnp.bfloat16), "col", scatter_dimension=1, tiled=True
    ).astype(jnp.float32)
    grad_out_weight = lax.psum_scatter(
        contract_rows(act_full, grad_out).astype(jnp.bfloat16),
        "row",
        scatter_dimension=0,
        tiled=True,
    ).astype(jnp.float32)
    conv_grad = (act_grad * conv_sig * (1.0 + conv_pre * (1.0 - conv_sig))).astype(jnp.bfloat16)
    conv_wide = conv_grad.astype(jnp.float32)
    padded_grad = extended(conv_grad, (("row", 0),), half_width).astype(jnp.float32)
    outer_masks = tap_masks(
        row_start - half_width + jnp.arange(row_count + 2 * half_width, dtype=jnp.int32)
    )
    glu_grad = jnp.zeros((row_count, chan_count), jnp.float32)
    kernel_rows = []
    for tap_index in range(K):
        begin = 2 * half_width - tap_index
        glu_grad = (
            glu_grad
            + kernel[tap_index][None, :]
            * outer_masks[tap_index, begin : begin + row_count][:, None]
            * padded_grad[begin : begin + row_count]
        )
        kernel_rows.append(
            jnp.sum(
                local_masks[tap_index][:, None]
                * conv_wide
                * padded_glu[tap_index : tap_index + row_count],
                axis=0,
            )
        )
    kernel_term = jnp.stack(kernel_rows)
    bias_term = jnp.sum(conv_wide, axis=0)
    grad_kernel, grad_bias = lax.psum((kernel_term, bias_term), "row")
    value_grad = (glu_grad * gate_sig).astype(jnp.bfloat16)
    gate_grad = (glu_grad * value_pre * gate_sig * (1.0 - gate_sig)).astype(jnp.bfloat16)
    both_grads = jnp.concatenate([value_grad, gate_grad], axis=1)
    in_weight = lax.psum_scatter(
        contract_rows(normed, both_grads).astype(jnp.bfloat16),
        "row",
        scatter_dimension=0,
        tiled=True,
    ).astype(jnp.float32)
    grad_value = in_weight[:, :chan_count]
    grad_gate = in_weight[:, chan_count:]
    norm_terms = contract_cols(value_grad, value_full) + contract_cols(gate_grad, gate_full)
    normed_grad = lax.psum_scatter(
        norm_terms.astype(jnp.bfloat16), "col", scatter_dimension=1, tiled=True
    ).astype(jnp.float32)
    hat_grad = normed_grad * local_gain[None, :]
    first_sum, second_sum = lax.psum(
        (jnp.sum(hat_grad, axis=1), jnp.sum(hat_grad * centred, axis=1)), "col"
    )
    input_grad = (
        grad_out.astype(jnp.float32)
        + inv_std[:, None]
        * (hat_grad - first_sum[:, None] / width - centred * (second_sum / width)[:, None])
    ).astype(jnp.bfloat16)
    gain_term = jnp.sum(normed_grad * centred, axis=0)
    grad_gain = lax.psum(gain_term, "row")
    return (
        encoded,
        input_grad,
        grad_value,
        grad_gate,
        grad_kernel,
        grad_bias,
        grad_out_weight,
        grad_gain,
    )


def solution(mesh):
    placed = (
        P("row", "col"),
        P(),
        P("row", "col"),
        P("row", "col"),
        P(None, "col"),
        P("col"),
        P("row", "col"),
        P("row", "col"),
    )
    return jax.shard_map(
        shards,
        mesh=mesh,
        in_specs=placed,
        out_specs=(
            P("row", "col"),
            P("row", "col"),
            P("row", "col"),
            P("row", "col"),
            P(None, "col"),
            P("col"),
            P("row", "col"),
            P("col"),
        ),
        check_vma=False,
    )
```

profile of v0, /device:TPU:0, one launch (start us, length us, event | category | flops | bytes accessed | tf_op | source)
XLA Modules:
  0.0 864.5 jit_solution(822775014375690964)
XLA Ops:
  7.2 0.7 all-gather.14.cloned.1.call-update
  7.9 0.7 all-gather.10.cloned.1.call-update
  8.7 0.8 dynamic_slice.3
  9.5 1.1 convert_reduce_fusion.1
  10.5 76.2 %all-reduce.1 = (f32[384]{0:T(512)S(1)}, f32[384]{0:T(512)S(1)}) all-reduce(f32[384]{0:T(512)S(1)} %get-tuple-element.44, f32[384]{0:T(512)S(1)} %get-tuple-element.43), channel_id=1, replica_groups=mesh['row'=8,'col'=32] {'col'}, use_global_device_ids=true, to_apply=%region_3.0 | all-reduce | flops 768 | bytes 6144 | tf_op jit(solution)/shard_map/psum | solution.py:52
  86.8 0.6 copy-done.9
  87.3 1.7 fusion.16
  89.1 0.5 all-gather.8.cloned.1.call-update
  89.7 2.3 convolution_convert_fusion
  92.0 2.8 copy.16
  95.0 0.4 copy-done.69
  95.6 0.6 slice_bitcast_fusion.29
  96.2 0.7 slice_bitcast_fusion.30
  96.9 64.5 %all-gather.6.cloned.1.call-done = bf16[384,4096]{1,0:T(8,128)(2,1)} async-done(((bf16[384,128]{1,0:T(8,128)(2,1)}), bf16[384,4096]{1,0:T(8,128)(2,1)}) %all-gather.6.cloned.1.call-update) | async-done | bytes 3145744 | tf_op jit(solution)/shard_map/all_gather | solution.py:56
  161.4 3.3 fusion.2
  164.8 24.6 %all-gather.8.cloned.1.call-done = bf16[4096,128]{1,0:T(8,128)(2,1)} async-done(((bf16[512,128]{1,0:T(8,128)(2,1)}), bf16[4096,128]{1,0:T(8,128)(2,1)}) %all-gather.8.cloned.1.call-update) | async-done | bytes 1048592 | tf_op jit(solution)/shard_map/all_gather | solution.py:60
  189.4 2.9 multiply_convert_fusion.4
  192.3 2.2 collective-permute-start
  194.4 1.3 collective-permute-start.1
  195.9 1.6 collective-permute-done.1
  197.5 215.0 %reduce-scatter.13.cloned.1.call-done = bf16[128,384]{1,0:T(8,128)(2,1)} async-done(((bf16[4096,384]{1,0:T(8,128)(2,1)}), bf16[128,384]{1,0:T(8,128)(2,1)}) %reduce-scatter.13.cloned.1.call-update) | async-done | bytes 98320
  412.5 1.0 copy.17
  414.0 4.1 fusion.75
  418.1 0.7 multiply_convert_fusion.3
  419.2 1.3 collective-permute-start.2
  420.5 1.3 collective-permute-start.3
  421.9 3.3 collective-permute-done.3
  425.6 3.1 multiply_convert_fusion
  428.7 2.6 convolution_convert_fusion.1
  431.4 1.0 fusion.124
  432.7 1.0 add_convert_fusion
  433.6 2.9 copy.18
  436.8 58.9 %all-gather.12.cloned.1.call-done = bf16[384,4096]{1,0:T(8,128)(2,1)} async-done(((bf16[384,128]{1,0:T(8,128)(2,1)}), bf16[384,4096]{1,0:T(8,128)(2,1)}) %all-gather.12.cloned.1.call-update) | async-done | bytes 3145744 | tf_op jit(solution)/shard_map/all_gather | solution.py:79
  495.7 3.9 convolution_convert_fusion.2
  499.7 1.7 fusion.73
  501.4 1.9 fusion.77
  503.3 1.9 fusion.79
  505.1 3.0 stack.127
  508.1 26.7 %reduce-scatter.9.cloned.1.call-done = bf16[512,256]{1,0:T(8,128)(2,1)} async-done(((bf16[4096,256]{1,0:T(8,128)(2,1)}), bf16[512,256]{1,0:T(8,128)(2,1)}) %reduce-scatter.9.cloned.1.call-update) | async-done | bytes 262160 | tf_op jit(solution)/shard_map/reduce_scatter | solution.py:124
  534.8 1.8 fusion.121
  536.6 2.9 fusion.3
  539.5 218.2 %reduce-scatter.15.cloned.1.call-done = bf16[128,384]{1,0:T(8,128)(2,1)} async-done(((bf16[4096,384]{1,0:T(8,128)(2,1)}), bf16[128,384]{1,0:T(8,128)(2,1)}) %reduce-scatter.15.cloned.1.call-update) | async-done | bytes 98320
  757.7 1.0 copy.19
  758.7 0.3 fusion.12
  759.0 72.2 %all-reduce = (f32[384]{0:T(512)S(1)}, f32[384]{0:T(512)S(1)}) all-reduce(f32[384]{0:T(512)S(1)} %get-tuple-element.40, f32[384]{0:T(512)S(1)} %get-tuple-element.41), channel_id=1, replica_groups=mesh['row'=8,'col'=32] {'col'}, use_global_device_ids=true, to_apply=%region_9.10 | all-reduce | flops 768 | bytes 6144 | tf_op jit(solution)/shard_map/psum | solution.py:137
  831.2 24.2 %all-reduce.2 = (f32[31,128]{1,0:T(8,128)}, f32[128]{0:T(128)}, f32[128]{0:T(128)}) all-reduce(f32[31,128]{1,0:T(8,128)S(1)} %stack.127, f32[128]{0:T(128)S(1)} %copy-done.71, f32[128]{0:T(128)S(1)} %get-tuple-element.39), channel_id=1, replica_groups=mesh['row'=8,'col'=32] {'row'}, use_global_device_ids=true, to_apply=%region_42.43 | all-reduce | flops 4224 | bytes 33792 | tf_op jit(solution)/shard_map/psum | solution.py:120
  855.4 0.9 fusion.10
  856.3 1.6 convert_element_type.92
  (178 shorter events, 2.0 us)
Async XLA Ops:
  7.2 82.6 %all-gather.14.cloned.1.call-start = ((), (), s32[]{:S(2)}) async-start(), calls=%async_computation.8 | async-start | bytes 1179648 | tf_op jit(solution)/shard_map/all_gather | solution.py:80
  7.9 89.0 %all-gather.10.cloned.1.call-start = ((), (), s32[]{:S(2)}) async-start(), calls=%async_computation.6 | async-start | bytes 1179648 | tf_op jit(solution)/shard_map/all_gather | solution.py:61
  8.7 152.8 %all-gather.6.cloned.1.call-start = ((), (), s32[]{:S(2)}) async-start(), calls=%async_computation.4 | async-start | bytes 3244032 | tf_op jit(solution)/shard_map/all_gather | solution.py:56
  9.5 80.2 %copy-start.36 = (f32[128]{0:T(128)}, f32[128]{0:T(128)S(1)}, u32[]{:S(2)}) copy-start(f32[128]{0:T(128)S(1)} %dynamic_slice.3) | copy-start | bytes 1540
  89.1 100.3 %all-gather.8.cloned.1.call-start = ((), (), s32[]{:S(2)}) async-start(), calls=%async_computation.5 | async-start | bytes 1179648 | tf_op jit(solution)/shard_map/all_gather | solution.py:60
  89.6 322.9 %reduce-scatter.13.cloned.1.call-start = ((), (), s32[]{:S(2)}) async-start(), calls=%async_computation.11 | async-start | bytes 3244032
  94.8 400.9 %all-gather.12.cloned.1.call-start = ((), (), s32[]{:S(2)}) async-start(), calls=%async_computation.7 | async-start | bytes 3244032 | tf_op jit(solution)/shard_map/all_gather | solution.py:79
  95.5 318.0 %copy-start.13 = (f32[384]{0:T(512)}, f32[384]{0:T(512)S(1)}, u32[]{:S(2)}) copy-start(f32[384]{0:T(512)S(1)} %get-tuple-element.77) | copy-start | bytes 4612
  95.5 318.0 %copy-start.14 = (f32[384]{0:T(512)}, f32[384]{0:T(512)S(1)}, u32[]{:S(2)}) copy-start(f32[384]{0:T(512)S(1)} %get-tuple-element.78) | copy-start | bytes 4612
  95.5 318.0 %copy-start.15 = (f32[384]{0:T(512)}, f32[384]{0:T(512)S(1)}, u32[]{:S(2)}) copy-start(f32[384]{0:T(512)S(1)} %get-tuple-element.91) | copy-start | bytes 4612
  95.5 318.0 %copy-start.16 = (f32[384]{0:T(512)}, f32[384]{0:T(512)S(1)}, u32[]{:S(2)}) copy-start(f32[384]{0:T(512)S(1)} %get-tuple-element.92) | copy-start | bytes 4612
  95.5 318.0 %copy-start.17 = (f32[384]{0:T(512)}, f32[384]{0:T(512)S(1)}, u32[]{:S(2)}) copy-start(f32[384]{0:T(512)S(1)} %get-tuple-element.93) | copy-start | bytes 4612
  95.5 318.0 %copy-start.18 = (f32[384]{0:T(512)}, f32[384]{0:T(512)S(1)}, u32[]{:S(2)}) copy-start(f32[384]{0:T(512)S(1)} %get-tuple-element.94) | copy-start | bytes 4612
  95.5 318.0 %copy-start.19 = (f32[384]{0:T(512)}, f32[384]{0:T(512)S(1)}, u32[]{:S(2)}) copy-start(f32[384]{0:T(512)S(1)} %get-tuple-element.76) | copy-start | bytes 4612
  95.6 318.0 %copy-start.20 = (f32[384]{0:T(512)}, f32[384]{0:T(512)S(1)}, u32[]{:S(2)}) copy-start(f32[384]{0:T(512)S(1)} %get-tuple-element.80) | copy-start | bytes 4612
  95.6 318.0 %copy-start.21 = (f32[384]{0:T(512)}, f32[384]{0:T(512)S(1)}, u32[]{:S(2)}) copy-start(f32[384]{0:T(512)S(1)} %get-tuple-element.81) | copy-start | bytes 4612
  95.6 318.0 %copy-start.22 = (f32[384]{0:T(512)}, f32[384]{0:T(512)S(1)}, u32[]{:S(2)}) copy-start(f32[384]{0:T(512)S(1)} %get-tuple-element.82) | copy-start | bytes 4612
  96.2 317.4 %copy-start.38 = (f32[128]{0:T(128)}, f32[128]{0:T(128)S(1)}, u32[]{:S(2)}) copy-start(f32[128]{0:T(128)S(1)} %get-tuple-element.143) | copy-start | bytes 1540
  96.2 317.4 %copy-start.39 = (f32[128]{0:T(128)}, f32[128]{0:T(128)S(1)}, u32[]{:S(2)}) copy-start(f32[128]{0:T(128)S(1)} %get-tuple-element.144) | copy-start | bytes 1540
  96.2 317.4 %copy-start.40 = (f32[128]{0:T(128)}, f32[128]{0:T(128)S(1)}, u32[]{:S(2)}) copy-start(f32[128]{0:T(128)S(1)} %get-tuple-element.145) | copy-start | bytes 1540
  96.2 317.4 %copy-start.41 = (f32[128]{0:T(128)}, f32[128]{0:T(128)S(1)}, u32[]{:S(2)}) copy-start(f32[128]{0:T(128)S(1)} %get-tuple-element.146) | copy-start | bytes 1540
  96.2 317.4 %copy-start.42 = (f32[128]{0:T(128)}, f32[128]{0:T(128)S(1)}, u32[]{:S(2)}) copy-start(f32[128]{0:T(128)S(1)} %get-tuple-element.147) | copy-start | bytes 1540
  192.3 3.7 collective-permute-start
  194.4 3.1 collective-permute-start.1
  195.8 222.2 %copy-start.23 = (f32[384]{0:T(512)}, f32[384]{0:T(512)S(1)}, u32[]{:S(2)}) copy-start(f32[384]{0:T(512)S(1)} %get-tuple-element.95) | copy-start | bytes 4612
  195.8 222.2 %copy-start.24 = (f32[384]{0:T(512)}, f32[384]{0:T(512)S(1)}, u32[]{:S(2)}) copy-start(f32[384]{0:T(512)S(1)} %get-tuple-element.100) | copy-start | bytes 4612
  195.8 222.2 %copy-start.25 = (f32[384]{0:T(512)}, f32[384]{0:T(512)S(1)}, u32[]{:S(2)}) copy-start(f32[384]{0:T(512)S(1)} %get-tuple-element.101) | copy-start | bytes 4612
  195.8 222.2 %copy-start.26 = (f32[384]{0:T(512)}, f32[384]{0:T(512)S(1)}, u32[]{:S(2)}) copy-start(f32[384]{0:T(512)S(1)} %get-tuple-element.102) | copy-start | bytes 4612
  195.8 222.2 %copy-start.27 = (f32[384]{0:T(512)}, f32[384]{0:T(512)S(1)}, u32[]{:S(2)}) copy-start(f32[384]{0:T(512)S(1)} %get-tuple-element.103) | copy-start | bytes 4612
  195.8 222.2 %copy-start.28 = (f32[384]{0:T(512)}, f32[384]{0:T(512)S(1)}, u32[]{:S(2)}) copy-start(f32[384]{0:T(512)S(1)} %get-tuple-element.104) | copy-start | bytes 4612
  195.8 222.2 %copy-start.29 = (f32[384]{0:T(512)}, f32[384]{0:T(512)S(1)}, u32[]{:S(2)}) copy-start(f32[384]{0:T(512)S(1)} %get-tuple-element.105) | copy-start | bytes 4612
  195.9 222.2 %copy-start.30 = (f32[384]{0:T(512)}, f32[384]{0:T(512)S(1)}, u32[]{:S(2)}) copy-start(f32[384]{0:T(512)S(1)} %get-tuple-element.106) | copy-start | bytes 4612
  195.9 222.2 %copy-start.31 = (f32[384]{0:T(512)}, f32[384]{0:T(512)S(1)}, u32[]{:S(2)}) copy-start(f32[384]{0:T(512)S(1)} %get-tuple-element.96) | copy-start | bytes 4612
  195.9 222.2 %copy-start.32 = (f32[384]{0:T(512)}, f32[384]{0:T(512)S(1)}, u32[]{:S(2)}) copy-start(f32[384]{0:T(512)S(1)} %get-tuple-element.97) | copy-start | bytes 4612
  195.9 222.2 %copy-start.33 = (f32[384]{0:T(512)}, f32[384]{0:T(512)S(1)}, u32[]{:S(2)}) copy-start(f32[384]{0:T(512)S(1)} %get-tuple-element.98) | copy-start | bytes 4612
  195.9 222.2 %copy-start.34 = (f32[384]{0:T(512)}, f32[384]{0:T(512)S(1)}, u32[]{:S(2)}) copy-start(f32[384]{0:T(512)S(1)} %get-tuple-element.99) | copy-start | bytes 4612
  418.9 116.0 %reduce-scatter.9.cloned.1.call-start = ((), (), s32[]{:S(2)}) async-start(), calls=%async_computation.9 | async-start | bytes 2359296 | tf_op jit(solution)/shard_map/reduce_scatter | solution.py:124
  419.2 2.7 collective-permute-start.2
  420.5 4.8 collective-permute-start.3
  431.4 326.3 %reduce-scatter.15.cloned.1.call-start = ((), (), s32[]{:S(2)}) async-start(), calls=%async_computation.12 | async-start | bytes 3244032
  436.5 59.2 %copy-start.6 = (bf16[384,128]{1,0:T(8,128)(2,1)S(1)}, bf16[384,128]{1,0:T(8,128)(2,1)}, u32[]{:S(2)}) copy-start(bf16[384,128]{1,0:T(8,128)(2,1)} %param.15) | copy-start | bytes 294916
  436.6 419.8 %reduce-scatter.11.cloned.1.call-start = ((), (), s32[]{:S(2)}) async-start(), calls=%async_computation.10 | async-start | bytes 1179648 | tf_op jit(solution)/shard_map/reduce_scatter | solution.py:88
  499.6 37.0 %copy-start = (bf16[384,4096]{1,0:T(8,128)(2,1)S(1)}, bf16[384,4096]{1,0:T(8,128)(2,1)}, u32[]{:S(2)}) copy-start(bf16[384,4096]{1,0:T(8,128)(2,1)} %all-gather.12.cloned.1.call-done) | copy-start | bytes 9437188
  505.1 253.6 %copy-start.10 = (f32[384]{0:T(512)S(1)}, f32[384]{0:T(512)}, u32[]{:S(2)}) copy-start(f32[384]{0:T(512)} %copy-done.9) | copy-start | bytes 4612
  505.1 253.6 %copy-start.12 = (f32[384]{0:T(512)S(1)}, f32[384]{0:T(512)}, u32[]{:S(2)}) copy-start(f32[384]{0:T(512)} %copy-done.11) | copy-start | bytes 4612
  505.1 253.6 %copy-start.37 = (f32[128]{0:T(128)S(1)}, f32[128]{0:T(128)}, u32[]{:S(2)}) copy-start(f32[128]{0:T(128)} %copy-done.36) | copy-start | bytes 1540
  505.1 326.1 %copy-start.71 = (f32[128]{0:T(128)S(1)}, f32[128]{0:T(128)}, u32[]{:S(2)}) copy-start(f32[128]{0:T(128)} %get-tuple-element.42) | copy-start | bytes 1540
  505.1 350.3 %copy-start.7 = (bf16[384,128]{1,0:T(8,128)(2,1)S(1)}, bf16[384,128]{1,0:T(8,128)(2,1)}, u32[]{:S(2)}) copy-start(bf16[384,128]{1,0:T(8,128)(2,1)} %param.15) | copy-start | bytes 294916
  (37 other events, 393.1 us)
Sparse Core Ops, SparseCore 0:
  9.9 27.1 all-gather.13
  38.9 25.7 all-gather.9
  89.2 72.2 all-gather.5
  163.2 26.1 all-gather.7
  193.1 219.3 reduce-scatter.12
  419.0 76.6 all-gather.11
  498.4 36.3 reduce-scatter.8
  539.2 218.4 reduce-scatter.14
  760.2 32.8 reduce-scatter.10
where the time goes:
time: 865 us; the launch traced here: 864 us
  waiting for transfers between devices  615 us (71%)
  blocking collectives  173 us (20%)
  matrix products  19.8 us (2%)
  other arithmetic  19.2 us (2%)
  local copies, waits for them, and re-layouts  16.5 us (2%)
  between operations  15 us (2%)
    unnamed x11, waiting for transfers between devices  435 us
    psum x1, blocking collectives, shards(): lax.psum((jnp.sum(wide, axis=1), jnp.sum(wide * wide, axis=1)), 'col')  76.2 us
    psum x1, blocking collectives, shards(): lax.psum((jnp.sum(hat_grad, axis=1), jnp.sum(hat_grad * centred, axis=1))...  72.2 us
    all_gather x1, waiting for transfers between devices, shards(): lax.all_gather((centred * local_gain[None, :]).astype(jnp.bfloat16), 'col...  64.5 us
    all_gather x1, waiting for transfers between devices, shards(): act_full = lax.all_gather(activated, 'col', axis=1, tiled=True)  58.9 us
    reduce_scatter x1, waiting for transfers between devices, shards(): lax.psum_scatter(contract_rows(normed, both_grads).astype(jnp.bfloat16),...  26.7 us
    all_gather x1, waiting for transfers between devices, shards(): lax.all_gather(w_value, 'row', axis=0, tiled=True)  24.6 us
    psum x1, blocking collectives, shards(): grad_kernel, grad_bias = lax.psum((kernel_term, bias_term), 'row')  24.2 us
  transfers between devices with their start and end apart: 13, of which 8 were waited for; matrix products, arithmetic and copies ran while one was open for 5% of the time, Pallas kernels for 0%

commit v1 on v0

--- a/solution.py
+++ b/solution.py
@@ -6,6 +6,19 @@
 K = 31
 LEN = 2048
 epsilon = 1e-05
+
+
+def ring_gather(x, axis, dim):
+    ways = lax.axis_size(axis)
+    up = [(d, (d + 1) % ways) for d in range(ways)]
+    down = [(d, (d - 1) % ways) for d in range(ways)]
+    earlier, later = ([x], [x])
+    for _ in range(ways // 2):
+        earlier.append(lax.ppermute(earlier[-1], axis, up))
+    for _ in range((ways - 1) // 2):
+        later.append(lax.ppermute(later[-1], axis, down))
+    line = jnp.concatenate([*earlier[::-1], *later[1:]], axis=dim)
+    return jnp.roll(line, (lax.axis_index(axis) - ways // 2) * x.shape[dim], axis=dim)
 
 
 def extended(block, sides, width):
@@ -57,7 +70,7 @@
         (centred * local_gain[None, :]).astype(jnp.bfloat16), "col", axis=1, tiled=True
     )
     value_full, gate_full = (
-        lax.all_gather(w_value, "row", axis=0, tiled=True),
+        ring_gather(w_value, "row", 0),
         lax.all_gather(w_gate, "row", axis=0, tiled=True),
     )
     value_pre = jnp.dot(normed, value_full, preferred_element_type=jnp.float32)

time: 865 us -> 837 us (0.968)
  waiting for transfers between devices: 615 us -> 563 us
  local copies, waits for them, and re-layouts: 16.5 us -> 29.8 us
    all_gather x1, waiting for transfers between devices: 64.5 us -> 33.3 us  [shards(): lax.all_gather((centred * local_gain[None, :]).astype(jnp.bfloat16), 'col...]
    all_gather x1 -> x0, waiting for transfers between devices: 24.6 us -> none  [shards(): lax.all_gather(w_value, 'row', axis=0, tiled=True)]
    unnamed x148 -> x69, local copies, waits for them, and re-layouts: 9.21 us -> 20.8 us
    ppermute x0 -> x7, waiting for transfers between devices: none -> 11.4 us  [the longest x4 11.4 us: ring_gather(): earlier.append(lax.ppermute(earlier[-1], axis, up))]
    ppermute x0 -> x7, starting transfers between devices: none -> 8.88 us  [the longest x3 8.87 us: ring_gather(): later.append(lax.ppermute(later[-1], axis, down))]
    unnamed x11 -> x10, waiting for transfers between devices: 435 us -> 430 us
  transfers between devices with their start and end apart: 13 -> 19, of which waited for: 8 -> 11; matrix products, arithmetic and copies ran while one was open for 5% -> 7% of each run, Pallas kernels for 0% -> 0%
where the time goes in v1:
time: 837 us; the launch traced here: 836 us
  waiting for transfers between devices  563 us (67%)
  blocking collectives  173 us (21%)
  local copies, waits for them, and re-layouts  29.8 us (4%)
  matrix products  21.2 us (3%)
  other arithmetic  20.4 us (2%)
  starting transfers between devices  14.5 us (2%)
  between operations  14.5 us (2%)
    unnamed x10, waiting for transfers between devices  430 us
    psum x1, blocking collectives, shards(): lax.psum((jnp.sum(wide, axis=1), jnp.sum(wide * wide, axis=1)), 'col')  76.2 us
    psum x1, blocking collectives, shards(): lax.psum((jnp.sum(hat_grad, axis=1), jnp.sum(hat_grad * centred, axis=1))...  72.2 us
    all_gather x1, waiting for transfers between devices, shards(): act_full = lax.all_gather(activated, 'col', axis=1, tiled=True)  55.4 us
    all_gather x1, waiting for transfers between devices, shards(): lax.all_gather((centred * local_gain[None, :]).astype(jnp.bfloat16), 'col...  33.3 us
    reduce_scatter x1, waiting for transfers between devices, shards(): lax.psum_scatter(contract_rows(normed, both_grads).astype(jnp.bfloat16),...  27.3 us
    psum x1, blocking collectives, shards(): grad_kernel, grad_bias = lax.psum((kernel_term, bias_term), 'row')  24.2 us
    unnamed x69, local copies, waits for them, and re-layouts  20.8 us
  transfers between devices with their start and end apart: 19, of which 11 were waited for; matrix products, arithmetic and copies ran while one was open for 7% of the time, Pallas kernels for 0%

profile of v1, /device:TPU:0, one launch (start us, length us, event | category | flops | bytes accessed | tf_op | source)
XLA Modules:
  0.0 836.2 jit_solution(8200797047735621637)
XLA Ops:
  8.7 0.8 dynamic_slice.7
  9.5 1.1 convert_reduce_fusion.1
  10.5 76.2 %all-reduce.1 = (f32[384]{0:T(512)S(1)}, f32[384]{0:T(512)S(1)}) all-reduce(f32[384]{0:T(512)S(1)} %get-tuple-element.44, f32[384]{0:T(512)S(1)} %get-tuple-element.43), channel_id=1, replica_groups=mesh['row'=8,'col'=32] {'col'}, use_global_device_ids=true, to_apply=%region_3.0 | all-reduce | flops 768 | bytes 6144 | tf_op jit(solution)/shard_map/psum | solution.py:65
  87.3 1.7 fusion.19
  89.2 2.3 convolution_convert_fusion
  91.4 2.8 copy.16
  94.3 0.8 copy-done.9
  95.2 3.0 collective-permute-start.4
  98.1 2.6 collective-permute-done
  100.9 5.5 collective-permute-done.1
  107.0 3.0 collective-permute-start.5
  110.0 2.0 collective-permute-done.2
  113.3 3.0 collective-permute-start.6
  116.2 1.3 collective-permute-done.3
  128.1 33.3 %all-gather.5.cloned.1.call-done = bf16[384,4096]{1,0:T(8,128)(2,1)} async-done(((bf16[384,128]{1,0:T(8,128)(2,1)}), bf16[384,4096]{1,0:T(8,128)(2,1)}) %all-gather.5.cloned.1.call-update) | async-done | bytes 3145744 | tf_op jit(solution)/shard_map/all_gather | solution.py:69
  161.4 3.3 fusion.2
  164.8 3.0 multiply_convert_fusion.4
  167.7 1.3 collective-permute-start.7
  169.0 1.3 collective-permute-start.8
  171.0 2.8 collective-permute-done.8
  173.8 210.1 %reduce-scatter.13.cloned.1.call-done = bf16[128,384]{1,0:T(8,128)(2,1)} async-done(((bf16[4096,384]{1,0:T(8,128)(2,1)}), bf16[128,384]{1,0:T(8,128)(2,1)}) %reduce-scatter.13.cloned.1.call-update) | async-done | bytes 98320
  384.0 1.0 copy.17
  385.0 4.9 fusion.78
  390.7 0.8 fusion.117
  391.6 1.3 collective-permute-start.9
  392.9 1.3 collective-permute-start.10
  394.4 3.3 collective-permute-done.10
  397.7 3.5 multiply_convert_fusion.1
  401.9 2.6 convolution_convert_fusion.1
  404.6 1.1 copy-done.5
  405.7 1.0 fusion.129
  406.7 2.2 add_convert_fusion
  408.9 2.8 copy.18
  412.1 55.4 %all-gather.9.cloned.1.call-done = bf16[384,4096]{1,0:T(8,128)(2,1)} async-done(((bf16[384,128]{1,0:T(8,128)(2,1)}), bf16[384,4096]{1,0:T(8,128)(2,1)}) %all-gather.9.cloned.1.call-update) | async-done | bytes 3145744 | tf_op jit(solution)/shard_map/all_gather | solution.py:92
  467.5 4.0 convolution_convert_fusion.2
  471.5 0.8 fusion.76
  472.3 2.0 fusion.80
  474.3 1.9 fusion.82
  476.2 2.9 stack.127
  479.1 27.3 %reduce-scatter.9.cloned.1.call-done = bf16[512,256]{1,0:T(8,128)(2,1)} async-done(((bf16[4096,256]{1,0:T(8,128)(2,1)}), bf16[512,256]{1,0:T(8,128)(2,1)}) %reduce-scatter.9.cloned.1.call-update) | async-done | bytes 262160 | tf_op jit(solution)/shard_map/reduce_scatter | solution.py:137
  506.5 1.8 fusion.126
  508.3 2.9 fusion.3
  511.2 218.0 %reduce-scatter.15.cloned.1.call-done = bf16[128,384]{1,0:T(8,128)(2,1)} async-done(((bf16[4096,384]{1,0:T(8,128)(2,1)}), bf16[128,384]{1,0:T(8,128)(2,1)}) %reduce-scatter.15.cloned.1.call-update) | async-done | bytes 98320
  729.2 1.0 copy.19
  730.5 72.2 %all-reduce = (f32[384]{0:T(512)S(1)}, f32[384]{0:T(512)S(1)}) all-reduce(f32[384]{0:T(512)S(1)} %get-tuple-element.40, f32[384]{0:T(512)S(1)} %get-tuple-element.41), channel_id=1, replica_groups=mesh['row'=8,'col'=32] {'col'}, use_global_device_ids=true, to_apply=%region_9.10 | all-reduce | flops 768 | bytes 6144 | tf_op jit(solution)/shard_map/psum | solution.py:150
  802.7 24.2 %all-reduce.2 = (f32[31,128]{1,0:T(8,128)}, f32[128]{0:T(128)}, f32[128]{0:T(128)}) all-reduce(f32[31,128]{1,0:T(8,128)S(1)} %stack.127, f32[128]{0:T(128)S(1)} %copy-done.24, f32[128]{0:T(128)S(1)} %get-tuple-element.39), channel_id=1, replica_groups=mesh['row'=8,'col'=32] {'row'}, use_global_device_ids=true, to_apply=%region_42.43 | all-reduce | flops 4224 | bytes 33792 | tf_op jit(solution)/shard_map/psum | solution.py:133
  826.8 0.9 fusion.13
  827.8 1.6 convert_element_type.92
  (111 shorter events, 18.0 us)
Async XLA Ops:
  7.2 82.0 %all-gather.11.cloned.1.call-start = ((), (), s32[]{:S(2)}) async-start(), calls=%async_computation.7 | async-start | bytes 1179648 | tf_op jit(solution)/shard_map/all_gather | solution.py:93
  7.9 120.2 %all-gather.7.cloned.1.call-start = ((), (), s32[]{:S(2)}) async-start(), calls=%async_computation.5 | async-start | bytes 1179648 | tf_op jit(solution)/shard_map/all_gather | solution.py:74
  8.7 152.8 %all-gather.5.cloned.1.call-start = ((), (), s32[]{:S(2)}) async-start(), calls=%async_computation.4 | async-start | bytes 3244032 | tf_op jit(solution)/shard_map/all_gather | solution.py:69
  9.5 79.7 %copy-start.21 = (f32[128]{0:T(128)}, f32[128]{0:T(128)S(1)}, u32[]{:S(2)}) copy-start(f32[128]{0:T(128)S(1)} %dynamic_slice.7) | copy-start | bytes 1540
  86.7 0.6 copy-start.12
  86.7 0.6 copy-start.14
  89.1 294.9 %reduce-scatter.13.cloned.1.call-start = ((), (), s32[]{:S(2)}) async-start(), calls=%async_computation.10 | async-start | bytes 3244032
  94.2 0.9 copy-start.9
  94.2 12.1 %copy-start.20 = (f32[31,128]{1,0:T(8,128)S(1)}, f32[31,128]{1,0:T(8,128)}, u32[]{:S(2)}) copy-start(f32[31,128]{1,0:T(8,128)} %param.12) | copy-start | bytes 47620
  94.3 373.2 %all-gather.9.cloned.1.call-start = ((), (), s32[]{:S(2)}) async-start(), calls=%async_computation.6 | async-start | bytes 3244032 | tf_op jit(solution)/shard_map/all_gather | solution.py:92
  95.2 5.6 collective-permute-start
  95.2 11.9 %collective-permute-start.4 = (bf16[512,128]{1,0:T(8,128)(2,1)S(1)}, bf16[512,128]{1,0:T(8,128)(2,1)S(1)}, u32[]{:S(2)}, u32[]{:S(2)}) collective-permute-start(bf16[512,128]{1,0:T(8,128)(2,1)S(1)} %copy-done.9), channel_id=1, source_target_pairs={{0,224},{32,0},{64,32},{96,64},{128,96},{160,128},{192,160},{224,1... | collective-permute-start | bytes 393224 | tf_op jit(solution)/shard_map/ppermute | solution.py:19
  98.1 2.7 copy-start.23
  100.8 5.6 collective-permute-start.1
  106.4 5.6 collective-permute-start.2
  107.0 6.2 collective-permute-start.5
  112.0 5.6 collective-permute-start.3
  113.3 8.9 %collective-permute-start.6 = (bf16[512,128]{1,0:T(8,128)(2,1)S(1)}, bf16[512,128]{1,0:T(8,128)(2,1)S(1)}, u32[]{:S(2)}, u32[]{:S(2)}) collective-permute-start(bf16[512,128]{1,0:T(8,128)(2,1)S(1)} %collective-permute-done.5), channel_id=1, source_target_pairs={{0,224},{32,0},{64,32},{96,64},{128,96},{160,128},{192,160},{224,1... | collective-permute-start | bytes 393224 | tf_op jit(solution)/shard_map/ppermute | solution.py:19
  161.4 3.3 copy-start.1
  164.8 6.2 copy-start.3
  167.7 3.3 collective-permute-start.7
  169.0 4.8 collective-permute-start.8
  390.6 115.8 %reduce-scatter.9.cloned.1.call-start = ((), (), s32[]{:S(2)}) async-start(), calls=%async_computation.8 | async-start | bytes 2359296 | tf_op jit(solution)/shard_map/reduce_scatter | solution.py:137
  391.6 2.7 collective-permute-start.9
  392.9 4.7 collective-permute-start.10
  397.7 3.5 copy-start.4
  397.7 3.5 copy-start.8
  401.2 0.6 copy-start.10
  404.5 1.2 copy-start.5
  404.5 324.6 %reduce-scatter.15.cloned.1.call-start = ((), (), s32[]{:S(2)}) async-start(), calls=%async_computation.11 | async-start | bytes 3244032
  405.7 1.0 copy-start.11
  411.8 55.7 %copy-start.6 = (bf16[384,128]{1,0:T(8,128)(2,1)S(1)}, bf16[384,128]{1,0:T(8,128)(2,1)}, u32[]{:S(2)}) copy-start(bf16[384,128]{1,0:T(8,128)(2,1)} %param.15) | copy-start | bytes 294916
  411.8 59.7 %copy-start.16 = (f32[384]{0:T(512)S(1)}, f32[384]{0:T(512)}, u32[]{:S(2)}) copy-start(f32[384]{0:T(512)} %get-tuple-element.76) | copy-start | bytes 4612
  411.8 59.6 %copy-start.17 = (f32[384]{0:T(512)S(1)}, f32[384]{0:T(512)}, u32[]{:S(2)}) copy-start(f32[384]{0:T(512)} %get-tuple-element.80) | copy-start | bytes 4612
  411.8 59.6 %copy-start.18 = (f32[384]{0:T(512)S(1)}, f32[384]{0:T(512)}, u32[]{:S(2)}) copy-start(f32[384]{0:T(512)} %get-tuple-element.81) | copy-start | bytes 4612
  411.8 59.6 %copy-start.19 = (f32[384]{0:T(512)S(1)}, f32[384]{0:T(512)}, u32[]{:S(2)}) copy-start(f32[384]{0:T(512)} %get-tuple-element.82) | copy-start | bytes 4612
  411.8 415.9 %reduce-scatter.11.cloned.1.call-start = ((), (), s32[]{:S(2)}) async-start(), calls=%async_computation.9 | async-start | bytes 1179648 | tf_op jit(solution)/shard_map/reduce_scatter | solution.py:101
  472.3 36.0 %copy-start = (bf16[384,4096]{1,0:T(8,128)(2,1)S(1)}, bf16[384,4096]{1,0:T(8,128)(2,1)}, u32[]{:S(2)}) copy-start(bf16[384,4096]{1,0:T(8,128)(2,1)} %all-gather.9.cloned.1.call-done) | copy-start | bytes 9437188
  472.3 36.0 %copy-start.2 = (bf16[384,128]{1,0:T(8,128)(2,1)S(1)}, bf16[384,128]{1,0:T(8,128)(2,1)}, u32[]{:S(2)}) copy-start(bf16[384,128]{1,0:T(8,128)(2,1)} %param.8) | copy-start | bytes 294916
  508.3 221.9 %copy-start.13 = (f32[384]{0:T(512)S(1)}, f32[384]{0:T(512)}, u32[]{:S(2)}) copy-start(f32[384]{0:T(512)} %copy-done.12) | copy-start | bytes 4612
  508.3 221.9 %copy-start.15 = (f32[384]{0:T(512)S(1)}, f32[384]{0:T(512)}, u32[]{:S(2)}) copy-start(f32[384]{0:T(512)} %copy-done.14) | copy-start | bytes 4612
  508.3 221.9 %copy-start.22 = (f32[128]{0:T(128)S(1)}, f32[128]{0:T(128)}, u32[]{:S(2)}) copy-start(f32[128]{0:T(128)} %copy-done.21) | copy-start | bytes 1540
  508.3 294.4 %copy-start.24 = (f32[128]{0:T(128)S(1)}, f32[128]{0:T(128)}, u32[]{:S(2)}) copy-start(f32[128]{0:T(128)} %get-tuple-element.42) | copy-start | bytes 1540
  508.3 318.5 %copy-start.7 = (bf16[384,128]{1,0:T(8,128)(2,1)S(1)}, bf16[384,128]{1,0:T(8,128)(2,1)}, u32[]{:S(2)}) copy-start(bf16[384,128]{1,0:T(8,128)(2,1)} %param.15) | copy-start | bytes 294916
Sparse Core Ops, SparseCore 0:
  9.9 27.1 all-gather.10
  38.9 25.7 all-gather.6
  89.2 72.2 all-gather.4
  165.2 218.7 reduce-scatter.12
  390.8 76.6 all-gather.8
  470.0 36.3 reduce-scatter.8
  510.8 218.2 reduce-scatter.14
  731.7 32.9 reduce-scatter.10
